TPU v7x, 32 devices: a whole 2x2x4 slice. The times are simulated.
32 devices in a mesh: rows: 16 (over z, y, core), heads: 2 (over x).
Axes of the slice: x: 2, y: 2, z: 4, core: 2. Of those that a mesh axis runs over, the one named last changes fastest.
Arguments:
- features: bfloat16 [8192, 1664], P(('rows', 'heads')), may hold values from -6 to 6
- segment_ids: int32 [8192], P(('rows', 'heads')), may hold values from 0 to 1, as said below
- padding_mask: int32 [8192], P(('rows', 'heads')), may hold values from 0 to 1, as said below
- w_proj: bfloat16 [1664, 1024], replicated, may hold values from -0.15625 to 0.15625
- proj_bias: float32 [1024], replicated, may hold values from -3 to 3
- gain_attn: float32 [1024], replicated, may hold values from 0.1 to 1.9
- w_qkv: bfloat16 [1024, 3, 1024], P(None, None, 'heads'), may hold values from -0.09375 to 0.09375
- w_out: bfloat16 [1024, 1024], P('heads'), may hold values from -3 to 3
- gain_ffn: float32 [1024], replicated, may hold values from 0.1 to 1.9
- w_gate_up: bfloat16 [1024, 2, 2816], P(None, None, 'heads'), may hold values from -0.1875 to 0.1875
- w_down: bfloat16 [2816, 1024], P('heads'), may hold values from -0.109375 to 0.109375
- cotangent: bfloat16 [8192, 1024], P(('rows', 'heads')), may hold values from -6 to 6
Outputs:
- layer_out: bfloat16 [8192, 1024], P(('rows', 'heads'))
- grad_features: float32 [8192, 1664], P(('rows', 'heads'))
- grad_proj: float32 [1664, 1024], replicated
- grad_bias: float32 [1024], replicated
- grad_gain_attn: float32 [1024], replicated
- grad_qkv: float32 [1024, 3, 1024], P(None, None, 'heads')
- grad_out: float32 [1024, 1024], P('heads')
- grad_gain_ffn: float32 [1024], replicated
- grad_gate_up: float32 [1024, 2, 2816], P(None, None, 'heads')
- grad_down: float32 [2816, 1024], P('heads')
Inputs may be any that keep to these rules, and one draw needn't show every extreme that they name: `segment_ids`: within each aligned block of 512 tokens (one packed row) the ids start at 0 and never fall; each pair holds 256 patches followed by its text, and the padding at a row's end has one id of its own. `padding_mask`: in each packed row the ones form a leading run that ends where the row's last whole pair ends; the rest is 0.
All inputs are finite; a program needn't handle non-finite values.
Results may differ from a plain program's by a relative error of at most 0.024.
Values may be sent and summed in bfloat16 or wider, within the bound.
No kernel may reach another device: no remote copies, remote signals or barrier semaphores. Data moves between devices by JAX's collectives and lax.ppermute only.
A program may use at most 128 MiB of HBM per device.

v0:
```python
import jax
import jax.numpy as jnp
from jax import lax
from jax.sharding import PartitionSpec as P

HEAD_DIM = 64
LEN_MAX = 2048
EPSILON = 1e-06
MASKED = -1000000000.0


def gelu_tanh(values):
    return jax.nn.gelu(values, approximate=True)


def contract(left, right, left_dim, right_dim):
    return lax.dot_general(
        left, right, (((left_dim,), (right_dim,)), ((), ())), preferred_element_type=jnp.float32
    )


def rms_forward(values, gain):
    scale = lax.rsqrt(jnp.mean(values * values, axis=-1, keepdims=True) + EPSILON)
    return (values * scale * gain, scale)


def rms_backward(values, scale, gain, grad_normed):
    unit = values * scale
    grad_unit = grad_normed * gain
    grad_values = scale * (grad_unit - unit * jnp.mean(grad_unit * unit, axis=-1, keepdims=True))
    return (grad_values, jnp.sum(grad_normed * unit, axis=0))


def block_scores(
    queries, key_rows, segments, padding, query_start, row_start, query_count, seq_len
):
    query_block = lax.dynamic_slice_in_dim(queries, query_start, query_count, 0)
    scores = jnp.einsum("qhd,khd->hqk", query_block, key_rows, preferred_element_type=jnp.float32)
    query_segment = lax.dynamic_slice_in_dim(segments, query_start, query_count, 0)
    query_place = query_start + jnp.arange(query_count)
    key_place = row_start + jnp.arange(seq_len)
    allowed = (query_segment[:, None] == segments[None, :]) & (
        (padding[None, :] == 1) | (query_place[:, None] == key_place[None, :])
    )
    return (jnp.where(allowed[None], scores, MASKED), query_block, key_rows)


def attention_forward(queries, key_rows, value_rows, segments, padding, seq_len, query_count):
    group_tokens = queries.shape[0]
    per_seq = seq_len // query_count

    def one_block(number):
        query_start = number * query_count
        row_start = number // per_seq * seq_len
        scores, _, _ = block_scores(
            queries, key_rows, segments, padding, query_start, row_start, query_count, seq_len
        )
        top = jnp.max(scores, axis=-1, keepdims=True)
        expo = jnp.exp(scores - top)
        weight_sum = jnp.sum(expo, axis=-1, keepdims=True)
        probs = (expo / weight_sum).astype(jnp.bfloat16)
        mixed = jnp.einsum("hqk,khd->qhd", probs, value_rows, preferred_element_type=jnp.float32)
        return (mixed.astype(jnp.bfloat16), (top + jnp.log(weight_sum))[:, :, 0])

    mixed, log_sums = lax.map(one_block, jnp.arange(group_tokens // query_count))
    return (mixed.reshape(group_tokens, -1), log_sums)


def attention_backward(
    queries, key_rows, value_rows, segments, padding, log_sums, grad_mixed, seq_len, query_count
):
    group_tokens, heads_here, head_size = queries.shape
    per_seq = seq_len // query_count

    def one_block(carry, item):
        grad_keys, grad_values = carry
        number, log_sum = item
        query_start = number * query_count
        row_start = number // per_seq * seq_len
        scores, query_block, key_block = block_scores(
            queries, key_rows, segments, padding, query_start, row_start, query_count, seq_len
        )
        grad_block = lax.dynamic_slice_in_dim(grad_mixed, query_start, query_count, 0)
        probs = jnp.exp(scores - log_sum[:, :, None])
        grad_probs = jnp.einsum(
            "qhd,khd->hqk", grad_block, value_rows, preferred_element_type=jnp.float32
        )
        grad_scores = probs * (grad_probs - jnp.sum(grad_probs * probs, axis=-1, keepdims=True))
        grad_scores = grad_scores.astype(jnp.bfloat16)
        grad_query = jnp.einsum(
            "hqk,khd->qhd", grad_scores, key_block, preferred_element_type=jnp.float32
        )
        key_part = jnp.einsum(
            "hqk,qhd->khd", grad_scores, query_block, preferred_element_type=jnp.float32
        )
        value_part = jnp.einsum(
            "hqk,qhd->khd",
            probs.astype(jnp.bfloat16),
            grad_block,
            preferred_element_type=jnp.float32,
        )
        grad_keys = grad_keys + key_part
        grad_values = grad_values + value_part
        return ((grad_keys, grad_values), grad_query)

    zero_grads = jnp.zeros((group_tokens, heads_here, head_size), jnp.float32)
    (grad_keys, grad_values), grad_queries = lax.scan(
        one_block, (zero_grads, zero_grads), (jnp.arange(group_tokens // query_count), log_sums)
    )
    return (grad_queries.reshape(group_tokens, heads_here, head_size), grad_keys, grad_values)


def local(
    features,
    segment_ids,
    padding_mask,
    w_proj,
    proj_bias,
    gain_attn,
    w_qkv,
    w_out,
    gain_ffn,
    w_gate_up,
    w_down,
    cotangent,
):
    local_tokens = features.shape[0]
    model_width = w_proj.shape[1]
    attn_cols = w_qkv.shape[2]
    heads_here = attn_cols // HEAD_DIM
    group_tokens = local_tokens * lax.axis_size("heads")
    seq_len = min(LEN_MAX, group_tokens)
    query_count = min(512, seq_len)
    qkv_flat = w_qkv.reshape(model_width, 3 * attn_cols)
    lifted = jnp.dot(features, w_proj, preferred_element_type=jnp.float32) + proj_bias
    normed, scale_attn = rms_forward(lifted, gain_attn)
    gathered, segments, padding = (
        lax.all_gather(normed.astype(jnp.bfloat16), "heads", axis=0, tiled=True),
        lax.all_gather(segment_ids, "heads", axis=0, tiled=True),
        lax.all_gather(padding_mask, "heads", axis=0, tiled=True),
    )
    projected = jnp.dot(gathered, qkv_flat, preferred_element_type=jnp.float32).astype(jnp.bfloat16)
    projected = projected.reshape(group_tokens, 3, heads_here, HEAD_DIM)
    queries, key_rows, value_rows = (projected[:, 0], projected[:, 1], projected[:, 2])
    mixed, log_sums = attention_forward(
        queries, key_rows, value_rows, segments, padding, seq_len, query_count
    )
    middle = lifted + lax.psum_scatter(
        jnp.dot(mixed, w_out, preferred_element_type=jnp.float32).astype(jnp.bfloat16),
        "heads",
        scatter_dimension=0,
        tiled=True,
    ).astype(jnp.float32)
    normed_ffn, scale_ffn = rms_forward(middle, gain_ffn)
    normed_ffn_b = normed_ffn.astype(jnp.bfloat16)
    ff_here = w_gate_up.shape[2]
    gathered_ffn = lax.all_gather(normed_ffn_b, "heads", axis=0, tiled=True)
    gate_flat = w_gate_up.reshape(model_width, 2 * ff_here)
    gate_up = jnp.dot(gathered_ffn, gate_flat, preferred_element_type=jnp.float32)
    activ, gelu_pull = jax.vjp(gelu_tanh, gate_up[:, :ff_here])
    up_part = gate_up[:, ff_here:]
    hidden = (activ * up_part).astype(jnp.bfloat16)
    layer_out = middle + lax.psum_scatter(
        jnp.dot(hidden, w_down, preferred_element_type=jnp.float32).astype(jnp.bfloat16),
        "heads",
        scatter_dimension=0,
        tiled=True,
    ).astype(jnp.float32)
    grad_gathered = lax.all_gather(cotangent, "heads", axis=0, tiled=True)
    grad_hidden = contract(grad_gathered, w_down, 1, 1)
    grad_pre = jnp.concatenate(
        [gelu_pull(grad_hidden * up_part)[0], grad_hidden * activ], axis=1
    ).astype(jnp.bfloat16)
    grad_gu_local = contract(gathered_ffn, grad_pre, 0, 0).reshape(model_width, 2, ff_here)
    grad_down_local = contract(hidden, grad_gathered, 0, 0)
    grad_normed_ffn = lax.psum_scatter(
        contract(grad_pre, gate_flat, 1, 1).astype(jnp.bfloat16),
        "heads",
        scatter_dimension=0,
        tiled=True,
    ).astype(jnp.float32)
    grad_gate_up, grad_down = (
        lax.psum(grad_gu_local.astype(jnp.bfloat16), "rows").astype(jnp.float32),
        lax.psum(grad_down_local.astype(jnp.bfloat16), "rows").astype(jnp.float32),
    )
    grad_ffn_norm, grad_gain_ffn = rms_backward(middle, scale_ffn, gain_ffn, grad_normed_ffn)
    grad_middle = cotangent.astype(jnp.float32) + grad_ffn_norm
    grad_mid_b = grad_middle.astype(jnp.bfloat16)
    grad_attn_in = lax.all_gather(grad_mid_b, "heads", axis=0, tiled=True)
    grad_mixed = contract(grad_attn_in, w_out, 1, 1).astype(jnp.bfloat16)
    grad_out_local = contract(mixed, grad_attn_in, 0, 0)
    grad_queries, grad_keys, grad_values = attention_backward(
        queries,
        key_rows,
        value_rows,
        segments,
        padding,
        log_sums,
        grad_mixed.reshape(group_tokens, heads_here, HEAD_DIM),
        seq_len,
        query_count,
    )
    grad_heads = (
        jnp.stack([grad_queries, grad_keys, grad_values], axis=1)
        .astype(jnp.bfloat16)
        .reshape(group_tokens, 3 * attn_cols)
    )
    grad_qkv_local = contract(gathered, grad_heads, 0, 0).reshape(model_width, 3, attn_cols)
    grad_normed = lax.psum_scatter(
        contract(grad_heads, qkv_flat, 1, 1).astype(jnp.bfloat16),
        "heads",
        scatter_dimension=0,
        tiled=True,
    ).astype(jnp.float32)
    grad_qkv, grad_out = (
        lax.psum(grad_qkv_local.astype(jnp.bfloat16), "rows").astype(jnp.float32),
        lax.psum(grad_out_local.astype(jnp.bfloat16), "rows").astype(jnp.float32),
    )
    grad_attn_norm, grad_gain_attn = rms_backward(lifted, scale_attn, gain_attn, grad_normed)
    grad_lifted = grad_middle + grad_attn_norm
    grad_lift_b = grad_lifted.astype(jnp.bfloat16)
    grad_features = contract(grad_lift_b, w_proj, 1, 1)
    grad_proj_local = contract(features, grad_lift_b, 0, 0)
    grad_proj, grad_bias, grad_gain_attn, grad_gain_ffn = lax.psum(
        (grad_proj_local, jnp.sum(grad_lifted, axis=0), grad_gain_attn, grad_gain_ffn),
        ("rows", "heads"),
    )
    return (
        layer_out.astype(jnp.bfloat16),
        grad_features,
        grad_proj,
        grad_bias,
        grad_gain_attn,
        grad_qkv,
        grad_out,
        grad_gain_ffn,
        grad_gate_up,
        grad_down,
    )


def solution(mesh):
    in_specs = (
        P(("rows", "heads"), None),
        P(("rows", "heads")),
        P(("rows", "heads")),
        P(),
        P(),
        P(),
        P(None, None, "heads"),
        P("heads", None),
        P(),
        P(None, None, "heads"),
        P("heads", None),
        P(("rows", "heads"), None),
    )
    out_specs = (
        P(("rows", "heads"), None),
        P(("rows", "heads"), None),
        P(),
        P(),
        P(),
        P(None, None, "heads"),
        P("heads", None),
        P(),
        P(None, None, "heads"),
        P("heads", None),
    )
    return jax.shard_map(local, mesh=mesh, in_specs=in_specs, out_specs=out_specs, check_vma=False)
```

profile of v0, /device:TPU:0, one launch (start us, length us, event | category | flops | bytes accessed | tf_op | source)
XLA Modules:
  0.0 693.1 jit_solution(15542330360389667371)
XLA Ops:
  13.5 5.1 all-gather.1
  28.6 9.0 %all-gather.7.cloned.1.call-done = bf16[512,1024]{1,0:T(8,128)(2,1)} async-done(((bf16[256,1024]{1,0:T(8,128)(2,1)}), bf16[512,1024]{1,0:T(8,128)(2,1)}) %all-gather.7.cloned.1.call-update) | async-done | bytes 1048592 | tf_op jit(solution)/shard_map/all_gather | solution.py:138
  37.6 5.2 convolution_convert_fusion.2
  57.5 20.4 %reduce-scatter.5.cloned.1.call-done = bf16[256,1024]{1,0:T(8,128)(2,1)} async-done(((bf16[512,1024]{1,0:T(8,128)(2,1)}), bf16[256,1024]{1,0:T(8,128)(2,1)}) %reduce-scatter.5.cloned.1.call-update) | async-done | bytes 524304 | tf_op jit(solution)/shard_map/reduce_scatter | solution.py:148
  83.0 6.2 copy.53
  89.1 14.2 %all-gather.9.cloned.1.call-done = bf16[512,1024]{1,0:T(8,128)(2,1)} async-done(((bf16[256,1024]{1,0:T(8,128)(2,1)}), bf16[512,1024]{1,0:T(8,128)(2,1)}) %all-gather.9.cloned.1.call-update) | async-done | bytes 1048592 | tf_op jit(solution)/shard_map/all_gather | solution.py:157
  103.3 8.7 %fusion.48 = f32[512,2816]{1,0:T(8,128)} fusion(bf16[512,1024]{1,0:T(8,128)(2,1)} %all-gather.9.cloned.1.call-done, bf16[1024,2816]{1,0:T(8,128)(2,1)} %bitcast.92), kind=kOutput, calls=%fused_computation.90 | convolution fusion | flops 2952790016 | bytes 12582912 | tf_op jit(solution)/shard_map/dot_general | solution.py:159
  112.0 14.2 %all-gather.11.cloned.1.call-done = bf16[512,1024]{1,0:T(8,128)(2,1)} async-done(((bf16[256,1024]{1,0:T(8,128)(2,1)}), bf16[512,1024]{1,0:T(8,128)(2,1)}) %all-gather.11.cloned.1.call-update) | async-done | bytes 1048592 | tf_op jit(solution)/shard_map/all_gather | solution.py:169
  126.1 8.8 %fusion.14 = (bf16[512,1408]{1,0:T(8,128)(2,1)S(1)}, bf16[512,1408]{1,0:T(8,128)(2,1)S(1)}, bf16[512,1408]{1,0:T(8,128)(2,1)}) fusion(f32[512,2816]{1,0:T(8,128)} %fusion.48, bf16[512,1024]{1,0:T(8,128)(2,1)} %all-gather.11.cloned.1.call-done, bf16[1408,1024]{1,0:T(8,128)(2,1)} %param.22), kind=kOutput, calls=%fused_computation.26 | convolution fusion | flops 1495138304 | bytes 14024704 | tf_op jit(solution)/shard_map/dot_general | solution.py:17
  140.7 20.4 %reduce-scatter.9.cloned.1.call-done = bf16[256,1024]{1,0:T(8,128)(2,1)} async-done(((bf16[512,1024]{1,0:T(8,128)(2,1)}), bf16[256,1024]{1,0:T(8,128)(2,1)}) %reduce-scatter.9.cloned.1.call-update) | async-done | bytes 524304 | tf_op jit(solution)/shard_map/reduce_scatter | solution.py:176
  166.3 21.2 %all-gather.13.cloned.1.call-done = bf16[512,1024]{1,0:T(8,128)(2,1)} async-done(((bf16[256,1024]{1,0:T(8,128)(2,1)}), bf16[512,1024]{1,0:T(8,128)(2,1)}) %all-gather.13.cloned.1.call-update) | async-done | bytes 1048592 | tf_op jit(solution)/shard_map/all_gather | solution.py:189
  189.9 5.5 fusion.17
  195.4 5.2 multiply_reduce_fusion
  215.9 15.3 %reduce-scatter.11.cloned.1.call-done = bf16[256,1024]{1,0:T(8,128)(2,1)} async-done(((bf16[512,1024]{1,0:T(8,128)(2,1)}), bf16[256,1024]{1,0:T(8,128)(2,1)}) %reduce-scatter.11.cloned.1.call-update) | async-done | bytes 524304 | tf_op jit(solution)/shard_map/reduce_scatter | solution.py:209
  233.1 21.4 %reduce-scatter.7.cloned.1.call-done = bf16[256,1024]{1,0:T(8,128)(2,1)} async-done(((bf16[512,1024]{1,0:T(8,128)(2,1)}), bf16[256,1024]{1,0:T(8,128)(2,1)}) %reduce-scatter.7.cloned.1.call-update) | async-done | bytes 524304 | tf_op jit(solution)/shard_map/reduce_scatter | solution.py:163
  263.2 7.9 %convolution_convert_fusion = bf16[1024,2816]{1,0:T(8,128)(2,1)} fusion(bf16[512,1024]{1,0:T(8,128)(2,1)} %all-gather.9.cloned.1.call-done, bf16[512,1408]{1,0:T(8,128)(2,1)} %copy-done.24, bf16[512,1408]{1,0:T(8,128)(2,1)} %copy-done.23), kind=kOutput, calls=%fused_computation.7 | convolution fusion | flops 2961440768 | bytes 9699328 | tf_op jit(solution)/shard_map/dot_general | solution.py:17
  271.0 12.1 %convert_element_type.141 = bf16[1024,2,1408]{2,1,0:T(2,128)(2,1)} reshape(bf16[1024,2816]{1,0:T(8,128)(2,1)} %convolution_convert_fusion) | data formatting | bytes 11534336 | tf_op jit(solution)/shard_map/convert_element_type | solution.py:183
  283.2 5.1 convolution_convert_fusion.1
  293.8 40.2 %all-reduce = (f32[1024]{0:T(1024)}, f32[1024]{0:T(1024)}, f32[1024]{0:T(1024)}) all-reduce(f32[1024]{0:T(1024)S(1)} %get-tuple-element.108, f32[1024]{0:T(1024)S(1)} %get-tuple-element.99, f32[1024]{0:T(1024)S(1)} %get-tuple-element.97), channel_id=1, replica_groups=mesh['rows'=16,'heads'=2] {'rows','heads'}, use_global_device_ids=true, to_apply=%region_13.14 | all-reduce | flops 3072 | bytes 24576 | tf_op jit(solution)/shard_map/psum | solution.py:224
  337.4 86.7 %all-reduce.5.cloned.1.call-done = f32[1664,1024]{0,1:T(8,128)} async-done(((f32[1664,1024]{0,1:T(8,128)}), f32[1664,1024]{0,1:T(8,128)}) %all-reduce.5.cloned.1.call-update) | async-done | bytes 6815760 | tf_op jit(solution)/shard_map/psum | solution.py:224
  424.1 7.6 %copy.46 = f32[1664,1024]{1,0:T(8,128)} copy(f32[1664,1024]{0,1:T(8,128)} %all-reduce.5.cloned.1.call-done) | data formatting | bytes 13631488
  431.7 238.1 %all-reduce.7.cloned.1.call-done = (bf16[1024,3,512]{2,0,1:T(8,128)(2,1)}, bf16[512,1024]{1,0:T(8,128)(2,1)}, bf16[1024,2,1408]{2,1,0:T(2,128)(2,1)}, bf16[1408,1024]{1,0:T(8,128)(2,1)}) async-done(((bf16[1024,3,512]{2,0,1:T(8,128)(2,1)}, bf16[512,1024]{1,0:T(8,128)(2,1)}, bf16[1024,2,1408]{2,1,0:T(2,128)(2,1)}, bf16[1408,1024]{1,0:T(8,128)(2,1)}), (bf16[1024,3,512]{2,0,1:T(8,128)(2,1)}, ...) | async-done | bytes 12845072 | tf_op jit(solution)/shard_map/psum | solution.py:216
  669.9 5.6 convert_element_type.137
  677.1 5.7 convert_element_type.142
  (117 shorter events, 88.4 us)
Async XLA Ops:
  7.2 5.3 copy-start.15
  7.2 6.3 copy-start.16
  7.2 30.4 %all-gather.7.cloned.1.call-start = ((), (), s32[]{:S(2)}) async-start(), calls=%async_computation.4 | async-start | bytes 1572864 | tf_op jit(solution)/shard_map/all_gather | solution.py:138
  13.5 64.4 %reduce-scatter.5.cloned.1.call-start = ((), (), s32[]{:S(2)}) async-start(), calls=%async_computation.5 | async-start | bytes 1572864 | tf_op jit(solution)/shard_map/reduce_scatter | solution.py:148
  18.7 4.7 copy-start.17
  54.9 24.6 %copy-start.14 = (f32[1024]{0:T(1024)S(1)}, f32[1024]{0:T(1024)}, u32[]{:S(2)}) copy-start(f32[1024]{0:T(1024)} %param.20) | copy-start | bytes 12292
  57.4 45.9 %all-gather.9.cloned.1.call-start = ((), (), s32[]{:S(2)}) async-start(), calls=%async_computation.6 | async-start | bytes 1572864 | tf_op jit(solution)/shard_map/all_gather | solution.py:157
  81.9 44.3 %all-gather.11.cloned.1.call-start = ((), (), s32[]{:S(2)}) async-start(), calls=%async_computation.8 | async-start | bytes 1572864 | tf_op jit(solution)/shard_map/all_gather | solution.py:169
  82.4 78.7 %reduce-scatter.9.cloned.1.call-start = ((), (), s32[]{:S(2)}) async-start(), calls=%async_computation.9 | async-start | bytes 1572864 | tf_op jit(solution)/shard_map/reduce_scatter | solution.py:176
  126.1 10.4 %copy-start.6 = (bf16[128,8,2,1408]{3,1,2,0:T(8,128)(2,1)S(1)}, bf16[128,8,2,1408]{3,1,2,0:T(8,128)(2,1)}, u32[]{:S(2)}) copy-start(bf16[128,8,2,1408]{3,1,2,0:T(8,128)(2,1)} %copy.53) | copy-start | bytes 17301508
  140.7 46.9 %all-gather.13.cloned.1.call-start = ((), (), s32[]{:S(2)}) async-start(), calls=%async_computation.10 | async-start | bytes 1572864 | tf_op jit(solution)/shard_map/all_gather | solution.py:189
  166.1 65.1 %reduce-scatter.11.cloned.1.call-start = ((), (), s32[]{:S(2)}) async-start(), calls=%async_computation.11 | async-start | bytes 1572864 | tf_op jit(solution)/shard_map/reduce_scatter | solution.py:209
  189.9 5.5 copy-start.3
  189.9 10.7 %slice-start = ((s8[8388608]{0:T(1024)(128)(4,1)}), s8[4194304]{0:T(1024)(128)(4,1)S(1)}, s32[]{:S(2)}) async-start(s8[8388608]{0:T(1024)(128)(4,1)} %bitcast.82), calls=%async_computation.14 | async-start | bytes 8388608
  195.4 5.2 slice-start.1
  210.7 43.7 %reduce-scatter.7.cloned.1.call-start = ((), (), s32[]{:S(2)}) async-start(), calls=%async_computation.7 | async-start | bytes 1572864 | tf_op jit(solution)/shard_map/reduce_scatter | solution.py:163
  215.8 208.3 %all-reduce.5.cloned.1.call-start = ((), (), s32[]{:S(2)}) async-start(), calls=%async_computation.12 | async-start | bytes 13631488 | tf_op jit(solution)/shard_map/psum | solution.py:224
  262.9 406.9 %all-reduce.7.cloned.1.call-start = ((), (), s32[]{:S(2)}) async-start(), calls=%async_computation.13 | async-start | bytes 25690112 | tf_op jit(solution)/shard_map/psum | solution.py:216
  283.1 5.1 copy-start.20
  283.1 5.1 copy-start.22
  669.9 7.2 %slice-start.2 = ((s8[5767168]{0:T(1024)(128)(4,1)}), s8[4194304]{0:T(1024)(128)(4,1)S(1)}, s32[]{:S(2)}) async-start(s8[5767168]{0:T(1024)(128)(4,1)} %bitcast.90), calls=%async_computation.16 | async-start | bytes 8388608
  669.9 5.7 copy-start.12
  669.9 7.2 %slice-start.3 = ((s8[5767168]{0:T(1024)(128)(4,1)}), s8[1572864]{0:T(1024)(128)(4,1)S(1)}, s32[]{:S(2)}) async-start(s8[5767168]{0:T(1024)(128)(4,1)} %bitcast.90), calls=%async_computation.17 | async-start | bytes 3145728
  677.1 5.8 copy-start.8
  (15 other events, 31.5 us)
Sparse Core Ops, SparseCore 0:
  13.6 23.9 all-gather.6
  57.6 20.3 reduce-scatter.4
  82.0 21.3 all-gather.8
  104.8 21.2 all-gather.10
  140.8 20.3 reduce-scatter.8
  166.2 21.2 all-gather.12
  210.9 20.3 reduce-scatter.10
  234.1 20.3 reduce-scatter.6
  263.0 161.0 all-reduce.4
  429.7 240.1 all-reduce.6
where the time goes:
time: 701 us; the launch traced here: 693 us
  waiting for transfers between devices  462 us (66%)
  matrix products  85.5 us (12%)
  blocking collectives  49.6 us (7%)
  local copies, waits for them, and re-layouts  43.6 us (6%)
  other arithmetic  36.7 us (5%)
  between operations  14.7 us (2%)
    psum x1, waiting for transfers between devices, local(): lax.psum(grad_qkv_local.astype(jnp.bfloat16), 'rows').astype(jnp.float32)  238 us
    psum x1, waiting for transfers between devices, local(): lax.psum((grad_proj_local, jnp.sum(grad_lifted, axis=0), grad_gain_attn,...  86.7 us
    dot_general x10, matrix products, contract(): lax.dot_general(left, right, (((left_dim,), (right_dim,)), ((), ())), pre...  43.7 us
    psum x1, blocking collectives, local(): lax.psum((grad_proj_local, jnp.sum(grad_lifted, axis=0), grad_gain_attn,...  40.2 us
    unnamed x61, local copies, waits for them, and re-layouts  28.9 us
    reduce_scatter x1, waiting for transfers between devices, local(): lax.psum_scatter(jnp.dot(hidden, w_down, preferred_element_type=jnp.float...  21.4 us
    all_gather x1, waiting for transfers between devices, local(): grad_attn_in = lax.all_gather(grad_mid_b, 'heads', axis=0, tiled=True)  21.2 us
    reduce_scatter x1, waiting for transfers between devices, local(): lax.psum_scatter(jnp.dot(mixed, w_out, preferred_element_type=jnp.float32...  20.4 us
  transfers between devices with their start and end apart: 10, of which 10 were waited for; matrix products, arithmetic and copies ran while one was open for 10% of the time, Pallas kernels for 0%

commit v1 on v0

--- a/solution.py
+++ b/solution.py
@@ -7,6 +7,12 @@
 LEN_MAX = 2048
 EPSILON = 1e-06
 MASKED = -1000000000.0
+
+
+def gather_and_add(x, name):
+    pieces = lax.all_gather(x, name, axis=0, tiled=False)
+    result = pieces.sum(axis=0)
+    return result
 
 
 def gelu_tanh(values):
@@ -213,7 +219,7 @@
         tiled=True,
     ).astype(jnp.float32)
     grad_qkv, grad_out = (
-        lax.psum(grad_qkv_local.astype(jnp.bfloat16), "rows").astype(jnp.float32),
+        gather_and_add(grad_qkv_local.astype(jnp.bfloat16), "rows").astype(jnp.float32),
         lax.psum(grad_out_local.astype(jnp.bfloat16), "rows").astype(jnp.float32),
     )
     grad_attn_norm, grad_gain_attn = rms_backward(lifted, scale_attn, gain_attn, grad_normed)

time: 701 us -> 905 us (1.29)
  waiting for transfers between devices: 462 us -> 643 us
  other arithmetic: 36.7 us -> 56.2 us
    all_gather x0 -> x1, waiting for transfers between devices: none -> 241 us  [gather_and_add(): pieces = lax.all_gather(x, name, axis=0, tiled=False)]
    psum x1, waiting for transfers between devices: 238 us -> 137 us  [local(): lax.psum(grad_out_local.astype(jnp.bfloat16), 'rows').astype(jnp.float32)]
    psum x1, waiting for transfers between devices: 86.7 us -> 155 us  [local(): lax.psum((grad_proj_local, jnp.sum(grad_lifted, axis=0), grad_gain_attn,...]
    reduce_sum x0 -> x1, other arithmetic: none -> 18.3 us  [gather_and_add(): result = pieces.sum(axis=0)]
    reduce_scatter x1, waiting for transfers between devices: 15.3 us -> 0.02 us  [local(): lax.psum_scatter(contract(grad_heads, qkv_flat, 1, 1).astype(jnp.bfloat16...]
    reduce_scatter x1, waiting for transfers between devices: 21.4 us -> 9.5 us  [local(): lax.psum_scatter(jnp.dot(hidden, w_down, preferred_element_type=jnp.float...]
    unnamed x61 -> x55, local copies, waits for them, and re-layouts: 28.9 us -> 28.7 us
  transfers between devices with their start and end apart: 10 -> 11, of which waited for: 10 -> 10; matrix products, arithmetic and copies ran while one was open for 10% -> 10% of each run, Pallas kernels for 0% -> 0%
where the time goes in v1:
time: 905 us; the launch traced here: 897 us
  waiting for transfers between devices  643 us (71%)
  matrix products  87.4 us (10%)
  other arithmetic  56.2 us (6%)
  blocking collectives  51.4 us (6%)
  local copies, waits for them, and re-layouts  43.4 us (5%)
  between operations  14.4 us (2%)
    all_gather x1, waiting for transfers between devices, gather_and_add(): pieces = lax.all_gather(x, name, axis=0, tiled=False)  241 us
    psum x1, waiting for transfers between devices, local(): lax.psum((grad_proj_local, jnp.sum(grad_lifted, axis=0), grad_gain_attn,...  155 us
    psum x1, waiting for transfers between devices, local(): lax.psum(grad_out_local.astype(jnp.bfloat16), 'rows').astype(jnp.float32)  137 us
    dot_general x10, matrix products, contract(): lax.dot_general(left, right, (((left_dim,), (right_dim,)), ((), ())), pre...  45.5 us
    psum x1, blocking collectives, local(): lax.psum((grad_proj_local, jnp.sum(grad_lifted, axis=0), grad_gain_attn,...  42 us
    unnamed x55, local copies, waits for them, and re-layouts  28.7 us
    all_gather x1, waiting for transfers between devices, local(): grad_attn_in = lax.all_gather(grad_mid_b, 'heads', axis=0, tiled=True)  21.2 us
    reduce_scatter x1, waiting for transfers between devices, local(): lax.psum_scatter(jnp.dot(mixed, w_out, preferred_element_type=jnp.float32...  20.4 us
  transfers between devices with their start and end apart: 11, of which 10 were waited for; matrix products, arithmetic and copies ran while one was open for 10% of the time, Pallas kernels for 0%

profile of v1, /device:TPU:0, one launch (start us, length us, event | category | flops | bytes accessed | tf_op | source)
XLA Modules:
  0.0 897.5 jit_solution(9307884641021011760)
XLA Ops:
  28.6 9.0 %all-gather.9.cloned.1.call-done = bf16[512,1024]{1,0:T(8,128)(2,1)} async-done(((bf16[256,1024]{1,0:T(8,128)(2,1)}), bf16[512,1024]{1,0:T(8,128)(2,1)}) %all-gather.9.cloned.1.call-update) | async-done | bytes 1048592 | tf_op jit(solution)/shard_map/all_gather | solution.py:144
  37.6 5.2 convolution_convert_fusion.2
  57.5 20.4 %reduce-scatter.5.cloned.1.call-done = bf16[256,1024]{1,0:T(8,128)(2,1)} async-done(((bf16[512,1024]{1,0:T(8,128)(2,1)}), bf16[256,1024]{1,0:T(8,128)(2,1)}) %reduce-scatter.5.cloned.1.call-update) | async-done | bytes 524304 | tf_op jit(solution)/shard_map/reduce_scatter | solution.py:154
  83.0 6.2 copy.53
  89.2 14.1 %all-gather.11.cloned.1.call-done = bf16[512,1024]{1,0:T(8,128)(2,1)} async-done(((bf16[256,1024]{1,0:T(8,128)(2,1)}), bf16[512,1024]{1,0:T(8,128)(2,1)}) %all-gather.11.cloned.1.call-update) | async-done | bytes 1048592 | tf_op jit(solution)/shard_map/all_gather | solution.py:163
  103.4 8.7 fusion.48
  112.0 14.2 %all-gather.13.cloned.1.call-done = bf16[512,1024]{1,0:T(8,128)(2,1)} async-done(((bf16[256,1024]{1,0:T(8,128)(2,1)}), bf16[512,1024]{1,0:T(8,128)(2,1)}) %all-gather.13.cloned.1.call-update) | async-done | bytes 1048592 | tf_op jit(solution)/shard_map/all_gather | solution.py:175
  126.2 8.8 fusion.14
  140.7 20.4 %reduce-scatter.9.cloned.1.call-done = bf16[256,1024]{1,0:T(8,128)(2,1)} async-done(((bf16[512,1024]{1,0:T(8,128)(2,1)}), bf16[256,1024]{1,0:T(8,128)(2,1)}) %reduce-scatter.9.cloned.1.call-update) | async-done | bytes 524304 | tf_op jit(solution)/shard_map/reduce_scatter | solution.py:182
  166.3 21.2 %all-gather.15.cloned.1.call-done = bf16[512,1024]{1,0:T(8,128)(2,1)} async-done(((bf16[256,1024]{1,0:T(8,128)(2,1)}), bf16[512,1024]{1,0:T(8,128)(2,1)}) %all-gather.15.cloned.1.call-update) | async-done | bytes 1048592 | tf_op jit(solution)/shard_map/all_gather | solution.py:195
  189.9 5.5 fusion.17
  195.4 5.2 multiply_reduce_fusion
  216.1 8.1 convolution_convert_fusion
  224.2 12.1 %convert_element_type.143 = bf16[1024,2,1408]{2,1,0:T(2,128)(2,1)} reshape(bf16[1024,2816]{1,0:T(8,128)(2,1)} %convolution_convert_fusion) | data formatting | bytes 11534336 | tf_op jit(solution)/shard_map/convert_element_type | solution.py:189
  244.9 9.5 %reduce-scatter.7.cloned.1.call-done = bf16[256,1024]{1,0:T(8,128)(2,1)} async-done(((bf16[512,1024]{1,0:T(8,128)(2,1)}), bf16[256,1024]{1,0:T(8,128)(2,1)}) %reduce-scatter.7.cloned.1.call-update) | async-done | bytes 524304 | tf_op jit(solution)/shard_map/reduce_scatter | solution.py:169
  263.0 5.2 convolution_convert_fusion.3
  268.2 42.0 %all-reduce = (f32[1024]{0:T(1024)}, f32[1024]{0:T(1024)}, f32[1024]{0:T(1024)}) all-reduce(f32[1024]{0:T(1024)S(1)} %get-tuple-element.107, f32[1024]{0:T(1024)S(1)} %get-tuple-element.99, f32[1024]{0:T(1024)S(1)} %get-tuple-element.97), channel_id=1, replica_groups=mesh['rows'=16,'heads'=2] {'rows','heads'}, use_global_device_ids=true, to_apply=%region_13.14 | all-reduce | flops 3072 | bytes 24576 | tf_op jit(solution)/shard_map/psum | solution.py:230
  313.5 137.3 %all-reduce.7.cloned.1.call-done = (bf16[512,1024]{1,0:T(8,128)(2,1)}, bf16[1024,2,1408]{2,1,0:T(2,128)(2,1)}, bf16[1408,1024]{1,0:T(8,128)(2,1)}) async-done(((bf16[512,1024]{1,0:T(8,128)(2,1)}, bf16[1024,2,1408]{2,1,0:T(2,128)(2,1)}, bf16[1408,1024]{1,0:T(8,128)(2,1)}), (bf16[512,1024]{1,0:T(8,128)(2,1)}, bf16[1024,2,1408]{2,1,0:T(2,128)(2,1)}, bf16[1408,1024]{1,0:T(8,128)(2,1)})) %all-reduce.7.cloned.1.call-update) | async-done | bytes 9699344 | tf_op jit(solution)/shard_map/psum | solution.py:223
  457.0 5.7 convert_element_type.144
  462.8 155.4 %all-reduce.5.cloned.1.call-done = f32[1664,1024]{0,1:T(8,128)} async-done(((f32[1664,1024]{0,1:T(8,128)}), f32[1664,1024]{0,1:T(8,128)}) %all-reduce.5.cloned.1.call-update) | async-done | bytes 6815760 | tf_op jit(solution)/shard_map/psum | solution.py:230
  618.2 7.6 copy.46
  625.8 241.1 %all-gather.17.cloned.1.call-done = bf16[16384,3,512]{2,0,1:T(8,128)(2,1)} async-done(((bf16[1024,3,512]{2,0,1:T(8,128)(2,1)}), bf16[16384,3,512]{2,0,1:T(8,128)(2,1)}) %all-gather.17.cloned.1.call-update) | async-done | bytes 50331664 | tf_op jit(solution)/shard_map/all_gather | solution.py:13
  866.9 18.3 %reduce_sum.103 = bf16[1024,3,512]{2,0,1:T(8,128)(2,1)} reduce(bf16[16,1024,3,512]{3,1,0,2:T(8,128)(2,1)} %bitcast.85, bf16[]{:T(256)} %constant.91.clone.1), dimensions={0}, to_apply=%region_16.17 | reduce | flops 23592960 | bytes 53477376 | tf_op jit(solution)/shard_map/reduce_sum | solution.py:14
  885.2 5.5 convert_element_type.139
  (115 shorter events, 96.4 us)
Async XLA Ops:
  7.2 5.3 copy-start.13
  7.2 6.3 copy-start.14
  7.2 30.4 %all-gather.9.cloned.1.call-start = ((), (), s32[]{:S(2)}) async-start(), calls=%async_computation.4 | async-start | bytes 1572864 | tf_op jit(solution)/shard_map/all_gather | solution.py:144
  13.5 64.5 %reduce-scatter.5.cloned.1.call-start = ((), (), s32[]{:S(2)}) async-start(), calls=%async_computation.5 | async-start | bytes 1572864 | tf_op jit(solution)/shard_map/reduce_scatter | solution.py:154
  18.7 4.7 copy-start.15
  51.5 4.2 copy-start.16
  55.0 24.6 %copy-start.12 = (f32[1024]{0:T(1024)S(1)}, f32[1024]{0:T(1024)}, u32[]{:S(2)}) copy-start(f32[1024]{0:T(1024)} %param.20) | copy-start | bytes 12292
  57.5 45.9 %all-gather.11.cloned.1.call-start = ((), (), s32[]{:S(2)}) async-start(), calls=%async_computation.6 | async-start | bytes 1572864 | tf_op jit(solution)/shard_map/all_gather | solution.py:163
  81.9 44.3 %all-gather.13.cloned.1.call-start = ((), (), s32[]{:S(2)}) async-start(), calls=%async_computation.8 | async-start | bytes 1572864 | tf_op jit(solution)/shard_map/all_gather | solution.py:175
  82.5 78.7 %reduce-scatter.9.cloned.1.call-start = ((), (), s32[]{:S(2)}) async-start(), calls=%async_computation.9 | async-start | bytes 1572864 | tf_op jit(solution)/shard_map/reduce_scatter | solution.py:182
  126.2 10.4 %copy-start.6 = (bf16[128,8,2,1408]{3,1,2,0:T(8,128)(2,1)S(1)}, bf16[128,8,2,1408]{3,1,2,0:T(8,128)(2,1)}, u32[]{:S(2)}) copy-start(bf16[128,8,2,1408]{3,1,2,0:T(8,128)(2,1)} %copy.53) | copy-start | bytes 17301508
  140.7 46.8 %all-gather.15.cloned.1.call-start = ((), (), s32[]{:S(2)}) async-start(), calls=%async_computation.10 | async-start | bytes 1572864 | tf_op jit(solution)/shard_map/all_gather | solution.py:195
  166.1 77.0 %reduce-scatter.11.cloned.1.call-start = ((), (), s32[]{:S(2)}) async-start(), calls=%async_computation.11 | async-start | bytes 1572864 | tf_op jit(solution)/shard_map/reduce_scatter | solution.py:215
  189.9 5.5 copy-start.3
  189.9 10.7 %slice-start = ((s8[8388608]{0:T(1024)(128)(4,1)}), s8[4194304]{0:T(1024)(128)(4,1)S(1)}, s32[]{:S(2)}) async-start(s8[8388608]{0:T(1024)(128)(4,1)} %bitcast.83), calls=%async_computation.15 | async-start | bytes 8388608
  195.4 5.2 slice-start.1
  210.7 43.7 %reduce-scatter.7.cloned.1.call-start = ((), (), s32[]{:S(2)}) async-start(), calls=%async_computation.7 | async-start | bytes 1572864 | tf_op jit(solution)/shard_map/reduce_scatter | solution.py:169
  215.8 235.0 %all-reduce.7.cloned.1.call-start = ((), (), s32[]{:S(2)}) async-start(), calls=%async_computation.14 | async-start | bytes 19398656 | tf_op jit(solution)/shard_map/psum | solution.py:223
  236.3 5.0 copy-start.17
  236.3 5.1 copy-start.19
  243.0 375.1 %all-reduce.5.cloned.1.call-start = ((), (), s32[]{:S(2)}) async-start(), calls=%async_computation.12 | async-start | bytes 13631488 | tf_op jit(solution)/shard_map/psum | solution.py:230
  254.5 4.4 copy-start.11
  262.9 604.0 %all-gather.17.cloned.1.call-start = ((), (), s32[]{:S(2)}) async-start(), calls=%async_computation.13 | async-start | bytes 53477376 | tf_op jit(solution)/shard_map/all_gather | solution.py:13
  450.8 6.2 slice-start.2
  (13 other events, 25.5 us)
Sparse Core Ops, SparseCore 0:
  13.6 23.9 all-gather.8
  57.6 20.3 reduce-scatter.4
  82.0 21.3 all-gather.10
  104.8 21.2 all-gather.12
  140.8 20.3 reduce-scatter.8
  166.2 21.2 all-gather.14
  210.8 20.3 reduce-scatter.10
  234.1 20.3 reduce-scatter.6
  259.6 191.1 all-reduce.6
  457.0 161.1 all-reduce.4
  619.7 247.1 all-gather.16
